TPU v7x, 512 devices: a whole 4x8x8 slice. The times are simulated.
512 devices in a mesh: dp: 8 (over z_lo, core), ctx: 64 (over z_hi, y, x).
Axes of the slice: x: 4, y: 8, z: 8 (z_hi: 2, z_lo: 4; z = z_hi * 4 + z_lo), core: 2. Of those that a mesh axis runs over, the one named last changes fastest.
Arguments:
- queries: bfloat16 [32768, 4096], P(('dp', 'ctx')), parts along dimension 0, as said below
- keys: bfloat16 [32768, 512], P(('dp', 'ctx')), parts along dimension 0, as said below
- values: bfloat16 [32768, 512], P(('dp', 'ctx')), parts along dimension 0, may hold values from -6 to 6
Outputs:
- attended: bfloat16 [32768, 4096], P(('dp', 'ctx')), parts along dimension 0
There are 8 independent parts, one for each index of `dp`. A program takes and returns all parts, laid end to end along the dimension named above; each array names one. Nothing has to cross between parts.
Inputs may be any that keep to these rules, and one draw needn't show every extreme that they name: `queries`: entries lie between -310 / sqrt(128) and 310 / sqrt(128). `keys`: entries lie between -6 and 6.
All inputs are finite; a program needn't handle non-finite values.
Results may differ from a plain program's by a relative error of at most 0.0035.
Values may be sent and summed in bfloat16 or wider, within the bound.
No kernel may reach another device: no remote copies, remote signals or barrier semaphores. Data moves between devices by JAX's collectives and lax.ppermute only.
A program may use at most 128 MiB of HBM per device.

v0:
```python
import math
import jax
import jax.numpy as jnp
from jax import lax
from jax.sharding import PartitionSpec as P

QH = 32
KVH = 4
HD = 128


def fresh_state(length, group_size):
    return (
        jnp.zeros((length, KVH, group_size, HD), jnp.float32),
        jnp.full((KVH, group_size, length), -1e30, jnp.float32),
        jnp.zeros((KVH, group_size, length), jnp.float32),
    )


def absorb(carry_state, query_block, query_pos, key_piece, value_piece):
    summed, running_max, denominator = carry_state
    key_heads = key_piece.reshape(key_piece.shape[0], KVH, HD)
    value_heads = value_piece.reshape(value_piece.shape[0], KVH, HD)
    scores = jnp.einsum(
        "tkgd,skd->kgts", query_block, key_heads, preferred_element_type=jnp.float32
    )
    scores = scores * (1.0 / math.sqrt(HD))
    key_pos = jnp.arange(key_heads.shape[0], dtype=jnp.int32)
    scores = jnp.where(key_pos[None, :] <= query_pos[:, None], scores, -jnp.inf)
    new_max = jnp.maximum(running_max, scores.max(-1))
    weights = jnp.exp(scores - new_max[..., None])
    denominator = weights.sum(-1)
    mixed_values = jnp.einsum(
        "kgts,skd->tkgd",
        weights.astype(jnp.bfloat16),
        value_heads,
        preferred_element_type=jnp.float32,
    )
    summed = mixed_values
    return (summed, new_max, denominator)


def guarded(carry_state, query_block, query_pos, key_piece, value_piece, offset):
    return lax.cond(
        offset <= query_pos[-1],
        lambda kept: absorb(kept, query_block, query_pos, key_piece, value_piece),
        lambda kept: kept,
        carry_state,
    )


def finish(carry_state):
    summed, running_max, denominator = carry_state
    result = summed / jnp.transpose(denominator, (2, 0, 1))[..., None]
    return result.reshape(summed.shape[0], QH * HD).astype(jnp.bfloat16)


def local(queries, keys, values):
    local_rows = queries.shape[0]
    my_index = lax.axis_index("ctx")
    group_size = QH // KVH
    own_pos = my_index * local_rows + jnp.arange(local_rows, dtype=jnp.int32)
    query_sets = ((queries.reshape(local_rows, KVH, group_size, HD), own_pos),)
    initial = tuple((fresh_state(entry[1].shape[0], group_size) for entry in query_sets))
    pieces = (
        lax.all_gather(keys, "ctx", axis=0, tiled=True),
        lax.all_gather(values, "ctx", axis=0, tiled=True),
    )
    offset = jnp.int32(0)
    states = tuple(
        (
            guarded(
                initial[number],
                query_sets[number][0],
                query_sets[number][1],
                pieces[0],
                pieces[1],
                offset,
            )
            for number in range(len(query_sets))
        )
    )
    return finish(states[0])


def solution(mesh):
    in_specs = (P(("dp", "ctx"), None), P(("dp", "ctx"), None), P(("dp", "ctx"), None))
    out_specs = P(("dp", "ctx"), None)
    return jax.shard_map(local, mesh=mesh, in_specs=in_specs, out_specs=out_specs, check_vma=False)
```

profile of v0, /device:TPU:2, one launch (start us, length us, event | category | flops | bytes accessed | tf_op | source)
XLA Modules:
  0.0 402.2 jit_solution(12471639932094628450)
XLA Ops:
  6.5 0.0 all-gather.3.cloned.1.call-start
  6.5 0.7 all-gather.3.cloned.1.call-update
  7.3 0.0 all-gather.5.cloned.1.call-start
  7.3 0.7 all-gather.5.cloned.1.call-update
  8.0 0.6 slice.3
  9.3 164.9 %all-gather.3.cloned.1.call-done = bf16[4096,512]{1,0:T(8,128)(2,1)} async-done(((bf16[64,512]{1,0:T(8,128)(2,1)}), bf16[4096,512]{1,0:T(8,128)(2,1)}) %all-gather.3.cloned.1.call-update) | async-done | bytes 4194320 | tf_op jit(solution)/shard_map/all_gather | solution.py:66
  174.2 156.1 %all-gather.5.cloned.1.call-done = bf16[4096,512]{1,0:T(8,128)(2,1)} async-done(((bf16[64,512]{1,0:T(8,128)(2,1)}), bf16[4096,512]{1,0:T(8,128)(2,1)}) %all-gather.5.cloned.1.call-update) | async-done | bytes 4194320 | tf_op jit(solution)/shard_map/all_gather | solution.py:67
  330.3 63.4 %conditional.1 = (f32[64,4,8,128]{3,0,2,1:T(8,128)S(1)}, f32[4,8,64]{2,1,0:T(8,128)S(1)}) conditional(s32[]{:T(128)} %bitcast.4, () %tuple.13, (s32[64]{0:T(128)S(1)}, bf16[4096,512]{1,0:T(8,128)(2,1)}, bf16[64,4096]{1,0:T(8,128)(2,1)}, bf16[4096,512]{1,0:T(8,128)(2,1)}) %tuple.14), branch_computations={%region_0.0_spmd, %region_1.4_spmd} | conditional | flops 4387502080 | bytes 129548560 | solution.py:44
  330.3 0.2 iota_compare_fusion
  330.5 6.9 %reshape.18 = bf16[4096,4,128]{2,1,0:T(4,128)(2,1)} reshape(bf16[4096,512]{1,0:T(8,128)(2,1)} %get-tuple-element.15) | data formatting | bytes 8388608 | tf_op jit(solution)/shard_map/cond/branch_1_fun/reshape | solution.py:22
  337.4 1.1 copy.15
  338.5 16.7 %fusion.2 = (f32[4,8,64]{2,1,0:T(8,128)S(1)}, f32[4,4096,64,8]{1,2,3,0:T(8,128)}) fusion(pred[64,4096]{1,0:T(8,128)(4,1)S(1)} %iota_compare_fusion, bf16[64,4,8,128]{3,2,1,0:T(8,128)(2,1)S(1)} %bitcast.27, bf16[4096,4,128,1]{2,1,0,3:T(4,128)(2,1)} %bitcast.25), kind=kOutput, calls=%fused_computation.4 | convolution fusion | flops 2172647424 | bytes 38543360 | tf_op jit(solution)/shard_map/cond/branch_1_fun/tkgd,skd->kgts/dot_general | solution.py:24
  355.2 15.4 %fusion = f32[4,8,64]{2,1,0:T(8,128)S(1)} fusion(f32[4,4096,64,8]{1,2,3,0:T(8,128)} %get-tuple-element.25, f32[4,8,64]{2,1,0:T(8,128)S(1)} %broadcast_maximum_fusion, pred[64,4096]{1,0:T(8,128)(4,1)S(1)} %iota_compare_fusion), kind=kLoop, calls=%fused_computation.2 | loop fusion | flops 33552384 | bytes 33832960 | tf_op jit(solution)/shard_map/cond/branch_1_fun/reduce_sum | solution.py:32
  370.5 6.9 %reshape.20 = bf16[4096,4,128]{2,1,0:T(4,128)(2,1)} reshape(bf16[4096,512]{1,0:T(8,128)(2,1)} %get-tuple-element.17) | data formatting | bytes 8388608 | tf_op jit(solution)/shard_map/cond/branch_1_fun/reshape | solution.py:23
  377.4 16.3 %fusion.9 = f32[64,4,8,128]{3,0,2,1:T(8,128)S(1)} fusion(bf16[4096,4,128,1]{2,1,0,3:T(4,128)(2,1)} %bitcast.26, f32[4,4096,64,8]{1,2,3,0:T(8,128)} %get-tuple-element.25, f32[4,8,64]{2,1,0:T(8,128)S(1)} %broadcast_maximum_fusion, pred[64,4096]{1,0:T(8,128)(4,1)S(1)} %iota_compare_fusion), kind=kOutput, calls=%fused_computation.10 | convolution fusion | flops 2181038080 | bytes 39067648 | tf_op jit(solution)/shard_map/cond/branch_1_fun/kgts,skd->tkgd/dot_general | solution.py:33
  393.7 0.3 divide_convert_fusion
  394.0 0.3 copy.8
  394.4 1.0 copy.30
  (2 shorter events, 0.0 us)
Async XLA Ops:
  6.5 167.6 %all-gather.3.cloned.1.call-start = ((), (), s32[]{:S(2)}) async-start(), calls=%async_computation | async-start | bytes 4259840 | tf_op jit(solution)/shard_map/all_gather | solution.py:66
  7.3 323.0 %all-gather.5.cloned.1.call-start = ((), (), s32[]{:S(2)}) async-start(), calls=%async_computation.1 | async-start | bytes 4259840 | tf_op jit(solution)/shard_map/all_gather | solution.py:67
Sparse Core Ops, SparseCore 0:
  11.8 162.2 all-gather.2
  178.7 151.5 all-gather.4
where the time goes:
time: 403 us; the launch traced here: 402 us
  waiting for transfers between devices  322 us (80%)
  matrix products  32.9 us (8%)
  local copies, waits for them, and re-layouts  16.8 us (4%)
  other arithmetic  15.9 us (4%)
  between operations  14.1 us (3%)
    all_gather x1, waiting for transfers between devices, local(): lax.all_gather(keys, 'ctx', axis=0, tiled=True)  165 us
    all_gather x1, waiting for transfers between devices, local(): lax.all_gather(values, 'ctx', axis=0, tiled=True)  156 us
    dot_general x1, matrix products, absorb(): jnp.einsum('tkgd,skd->kgts', query_block, key_heads, preferred_element_ty...  16.7 us
    dot_general x1, matrix products, absorb(): jnp.einsum('kgts,skd->tkgd', weights.astype(jnp.bfloat16), value_heads, p...  16.3 us
    reduce_sum x1, other arithmetic, absorb(): denominator = weights.sum(-1)  15.4 us
  transfers between devices with their start and end apart: 2, of which 2 were waited for; matrix products, arithmetic and copies ran while one was open for 0% of the time, Pallas kernels for 0%

commit v1 on v0

--- a/solution.py
+++ b/solution.py
@@ -64,7 +64,9 @@
     initial = tuple((fresh_state(entry[1].shape[0], group_size) for entry in query_sets))
     pieces = (
         lax.all_gather(keys, "ctx", axis=0, tiled=True),
-        lax.all_gather(values, "ctx", axis=0, tiled=True),
+        jnp.concatenate(
+            lax.all_to_all(jnp.stack([values] * lax.axis_size("ctx")), "ctx", 0, 0), axis=0
+        ),
     )
     offset = jnp.int32(0)
     states = tuple(

time: 403 us -> 331 us (0.82)
  waiting for transfers between devices: 322 us -> 228 us
  starting transfers between devices: 0.04 us -> 19.3 us
    all_gather x1 -> x0, waiting for transfers between devices: 156 us -> none  [local(): lax.all_gather(values, 'ctx', axis=0, tiled=True)]
    all_to_all x0 -> x1, waiting for transfers between devices: none -> 104 us  [local(): lax.all_to_all(jnp.stack([values] * lax.axis_size('ctx')), 'ctx', 0, 0)]
    all_gather x1, waiting for transfers between devices: 165 us -> 124 us  [local(): lax.all_gather(keys, 'ctx', axis=0, tiled=True)]
    all_to_all x0 -> x1, starting transfers between devices: none -> 19.3 us  [local(): lax.all_to_all(jnp.stack([values] * lax.axis_size('ctx')), 'ctx', 0, 0)]
    another operation x0 -> x2, local copies, waits for them, and re-layouts: none -> 10.2 us  [the longest x1 6.88 us: absorb(): value_heads = value_piece.reshape(value_piece.shape[0], KVH, HD)]
    reshape x1 -> x0, local copies, waits for them, and re-layouts: 6.87 us -> none  [absorb(): value_heads = value_piece.reshape(value_piece.shape[0], KVH, HD)]
where the time goes in v1:
time: 331 us
  waiting for transfers between devices  228 us (69%)
  matrix products  32.9 us (10%)
  local copies, waits for them, and re-layouts  20.1 us (6%)
  starting transfers between devices  19.3 us (6%)
  other arithmetic  15.9 us (5%)
  between operations  14.1 us (4%)
    all_gather x1, waiting for transfers between devices, local(): lax.all_gather(keys, 'ctx', axis=0, tiled=True)  124 us
    all_to_all x1, waiting for transfers between devices, local(): lax.all_to_all(jnp.stack([values] * lax.axis_size('ctx')), 'ctx', 0, 0)  104 us
    all_to_all x1, starting transfers between devices, local(): lax.all_to_all(jnp.stack([values] * lax.axis_size('ctx')), 'ctx', 0, 0)  19.3 us
    dot_general x1, matrix products, absorb(): jnp.einsum('tkgd,skd->kgts', query_block, key_heads, preferred_element_ty...  16.6 us
    dot_general x1, matrix products, absorb(): jnp.einsum('kgts,skd->tkgd', weights.astype(jnp.bfloat16), value_heads, p...  16.2 us
    reduce_sum x1, other arithmetic, absorb(): denominator = weights.sum(-1)  15.4 us
    reshape x1, local copies, waits for them, and re-layouts, absorb(): key_heads = key_piece.reshape(key_piece.shape[0], KVH, HD)  6.89 us
    another operation x1, local copies, waits for them, and re-layouts, absorb(): value_heads = value_piece.reshape(value_piece.shape[0], KVH, HD)  6.88 us
  transfers between devices with their start and end apart: 2, of which 2 were waited for; matrix products, arithmetic and copies ran while one was open for 0% of the time, Pallas kernels for 0%

profile of v1, /device:TPU:2, one launch (start us, length us, event | category | flops | bytes accessed | tf_op | source)
XLA Modules:
  0.0 330.6 jit_solution(17113282226564909740)
XLA Ops:
  6.5 3.3 stack.2
  9.8 19.3 %all-to-all-start = ((bf16[64,64,512]{2,1,0:T(8,128)(2,1)}), bf16[64,64,512]{2,1,0:T(8,128)(2,1)}, u32[]{:S(2)}, u32[]{:S(2)}) async-start(bf16[64,64,512]{2,1,0:T(8,128)(2,1)} %stack.2), calls=%async_computation | async-start | bytes 8388608 | tf_op jit(solution)/shard_map/all_to_all | solution.py:68
  29.1 0.0 all-gather.2.cloned.1.call-start
  29.2 0.7 all-gather.2.cloned.1.call-update
  29.9 0.6 slice.3
  31.1 104.0 %all-to-all-done = bf16[64,64,512]{2,1,0:T(8,128)(2,1)} async-done(((bf16[64,64,512]{2,1,0:T(8,128)(2,1)}), bf16[64,64,512]{2,1,0:T(8,128)(2,1)}, u32[]{:S(2)}, u32[]{:S(2)}) %all-to-all-start) | async-done | bytes 4194336 | tf_op jit(solution)/shard_map/all_to_all | solution.py:68
  135.1 123.7 %all-gather.2.cloned.1.call-done = bf16[4096,512]{1,0:T(8,128)(2,1)} async-done(((bf16[64,512]{1,0:T(8,128)(2,1)}), bf16[4096,512]{1,0:T(8,128)(2,1)}) %all-gather.2.cloned.1.call-update) | async-done | bytes 4194320 | tf_op jit(solution)/shard_map/all_gather | solution.py:66
  258.7 63.4 %conditional.1 = (f32[64,4,8,128]{3,0,2,1:T(8,128)S(1)}, f32[4,8,64]{2,1,0:T(8,128)S(1)}) conditional(s32[]{:T(128)} %bitcast.4, () %tuple.13, (s32[64]{0:T(128)S(1)}, bf16[4096,512]{1,0:T(8,128)(2,1)}, bf16[64,4096]{1,0:T(8,128)(2,1)}, bf16[64,64,512]{2,1,0:T(8,128)(2,1)}) %tuple.14), branch_computations={%region_0.0_spmd, %region_1.4_spmd} | conditional | flops 4387502080 | bytes 129548560 | solution.py:44
  258.7 0.2 iota_compare_fusion
  258.9 6.9 %reshape.18 = bf16[4096,4,128]{2,1,0:T(4,128)(2,1)} reshape(bf16[4096,512]{1,0:T(8,128)(2,1)} %get-tuple-element.15) | data formatting | bytes 8388608 | tf_op jit(solution)/shard_map/cond/branch_1_fun/reshape | solution.py:22
  265.8 1.1 copy.15
  267.0 16.6 %fusion.2 = (f32[4,8,64]{2,1,0:T(8,128)S(1)}, f32[4,4096,64,8]{1,2,3,0:T(8,128)}) fusion(pred[64,4096]{1,0:T(8,128)(4,1)S(1)} %iota_compare_fusion, bf16[64,4,8,128]{3,2,1,0:T(8,128)(2,1)S(1)} %bitcast.27, bf16[4096,4,128,1]{2,1,0,3:T(4,128)(2,1)} %bitcast.25), kind=kOutput, calls=%fused_computation.4 | convolution fusion | flops 2172647424 | bytes 38543360 | tf_op jit(solution)/shard_map/cond/branch_1_fun/tkgd,skd->kgts/dot_general | solution.py:24
  283.6 15.4 %fusion = f32[4,8,64]{2,1,0:T(8,128)S(1)} fusion(f32[4,4096,64,8]{1,2,3,0:T(8,128)} %get-tuple-element.25, f32[4,8,64]{2,1,0:T(8,128)S(1)} %broadcast_maximum_fusion, pred[64,4096]{1,0:T(8,128)(4,1)S(1)} %iota_compare_fusion), kind=kLoop, calls=%fused_computation.2 | loop fusion | flops 33552384 | bytes 33832960 | tf_op jit(solution)/shard_map/cond/branch_1_fun/reduce_sum | solution.py:32
  299.0 6.9 %reshape_reshape.2 = bf16[4096,4,128]{2,1,0:T(4,128)(2,1)} reshape(bf16[64,64,512]{2,1,0:T(8,128)(2,1)} %get-tuple-element.17) | data formatting | bytes 8388608 | tf_op jit(solution)/shard_map/cond/branch_1_fun/reshape;reshape | solution.py:23
  305.8 16.2 %fusion.9 = f32[64,4,8,128]{3,0,2,1:T(8,128)S(1)} fusion(bf16[4096,4,128,1]{2,1,0,3:T(4,128)(2,1)} %bitcast.26, f32[4,4096,64,8]{1,2,3,0:T(8,128)} %get-tuple-element.25, f32[4,8,64]{2,1,0:T(8,128)S(1)} %broadcast_maximum_fusion, pred[64,4096]{1,0:T(8,128)(4,1)S(1)} %iota_compare_fusion), kind=kOutput, calls=%fused_computation.10 | convolution fusion | flops 2181038080 | bytes 39067648 | tf_op jit(solution)/shard_map/cond/branch_1_fun/kgts,skd->tkgd/dot_general | solution.py:33
  322.1 0.3 divide_convert_fusion
  322.4 0.3 copy.8
  322.8 1.0 copy.30
  (2 shorter events, 0.0 us)
Async XLA Ops:
  9.8 125.3 %all-to-all-start = ((bf16[64,64,512]{2,1,0:T(8,128)(2,1)}), bf16[64,64,512]{2,1,0:T(8,128)(2,1)}, u32[]{:S(2)}, u32[]{:S(2)}) async-start(bf16[64,64,512]{2,1,0:T(8,128)(2,1)} %stack.2), calls=%async_computation | async-start | bytes 8388608 | tf_op jit(solution)/shard_map/all_to_all | solution.py:68
  29.1 229.6 %all-gather.2.cloned.1.call-start = ((), (), s32[]{:S(2)}) async-start(), calls=%async_computation.1 | async-start | bytes 4259840 | tf_op jit(solution)/shard_map/all_gather | solution.py:66
Sparse Core Ops, SparseCore 0:
  34.4 224.2 all-gather.1
